TPU v7x, 128 devices: a whole 4x4x4 slice. The times are simulated.
128 devices in a mesh: row: 8 (over y_lo, x), col: 16 (over z, y_hi, core).
Axes of the slice: x: 4, y: 4 (y_hi: 2, y_lo: 2; y = y_hi * 2 + y_lo), z: 4, core: 2. Of those that a mesh axis runs over, the one named last changes fastest.
Arguments:
- sources: bfloat16 [64, 32768], P(None, ('row', 'col')), may hold values from -6 to 6
- near_tiles: bfloat16 [128, 128, 256, 256], P('row', 'col'), may hold values from -0.03125 to 0.03125
- far_left: bfloat16 [128, 128, 32, 256], P('row', 'col'), may hold values from -1 to 1
- far_right: bfloat16 [128, 128, 32, 256], P('row', 'col'), may hold values from -0.03125 to 0.03125
- pattern: int32 [128, 128], P('row', 'col'), may hold values from 0 to 2
- band_end: int32 [128], P('row'), may hold values from 0 to 127, as said below
Outputs:
- image: float32 [64, 32768], P(None, ('row', 'col'))
Inputs may be any that keep to these rules, and one draw needn't show every extreme that they name: band_end[I] is at least I, so the band of every block-row starts at its own cluster; the bands of block-rows 0 to 15 run to the last cluster.
All inputs are finite; a program needn't handle non-finite values.
Results may differ from a plain program's by a relative error of at most 0.0021.
Values may be sent and summed in bfloat16 or wider, within the bound.
A program may use at most 128 MiB of HBM per device.

v0:
```python
import jax
import jax.numpy as jnp
from jax import lax
from jax.sharding import PartitionSpec as P


def shards(sources, near_tiles, far_left, far_right, pattern, band_end):
    row_count = lax.axis_size("row")
    col_count = lax.axis_size("col")
    row_index = lax.axis_index("row")
    col_index = lax.axis_index("col")
    num_cases = sources.shape[0]
    block_size = sources.shape[1]
    row_src = lax.all_gather(sources, "col", axis=1, tiled=True).reshape(
        num_cases, col_count, block_size
    )
    col_src = lax.all_gather(sources, "row", axis=1, tiled=True).reshape(
        num_cases, row_count, block_size
    )
    row_ids = row_index * col_count + jnp.arange(col_count, dtype=jnp.int32)
    col_ids = jnp.arange(row_count, dtype=jnp.int32) * col_count + col_index
    live = (row_ids[:, None] <= col_ids[None, :]) & (col_ids[None, :] <= band_end[:, None])
    near_mask = jnp.where(live & (pattern == 1), 1.0, 0.0).astype(jnp.float32)
    far_mask = jnp.where(live & (pattern == 2), 1.0, 0.0).astype(jnp.float32)
    near_rows = jnp.einsum(
        "ikab,ckb->cika", near_tiles, col_src, preferred_element_type=jnp.float32
    )
    far_coef = jnp.einsum(
        "ikrb,ckb->ikcr", far_right, col_src, preferred_element_type=jnp.float32
    ).astype(jnp.bfloat16)
    far_rows = jnp.einsum("ikra,ikcr->cika", far_left, far_coef, preferred_element_type=jnp.float32)
    row_part = jnp.sum(
        near_rows * near_mask[None, :, :, None] + far_rows * far_mask[None, :, :, None], axis=2
    )
    near_cols = jnp.einsum(
        "ikab,cia->ckib", near_tiles, row_src, preferred_element_type=jnp.float32
    )
    back_coef = jnp.einsum(
        "ikra,cia->ikcr", far_left, row_src, preferred_element_type=jnp.float32
    ).astype(jnp.bfloat16)
    far_cols = jnp.einsum(
        "ikrb,ikcr->ckib", far_right, back_coef, preferred_element_type=jnp.float32
    )
    col_part = jnp.sum(
        near_cols * near_mask.T[None, :, :, None] + far_cols * far_mask.T[None, :, :, None], axis=2
    )
    whole = jnp.zeros((num_cases, row_count, col_count, block_size), jnp.float32)
    whole = lax.dynamic_update_index_in_dim(whole, row_part, row_index, 1)
    column_hit = jnp.arange(col_count, dtype=jnp.int32)[None, None, :, None] == col_index
    whole = whole + jnp.where(column_hit, col_part[:, :, None, :], 0.0)
    result = lax.psum_scatter(
        whole.reshape(num_cases, row_count * col_count * block_size),
        ("row", "col"),
        scatter_dimension=1,
        tiled=True,
    )
    return result


def solution(mesh):
    placed = (
        P(None, ("row", "col")),
        P("row", "col", None, None),
        P("row", "col", None, None),
        P("row", "col", None, None),
        P("row", "col"),
        P("row"),
    )
    return jax.shard_map(
        shards, mesh=mesh, in_specs=placed, out_specs=P(None, ("row", "col")), check_vma=False
    )
```

profile of v0, /device:TPU:0, one launch (start us, length us, event | category | flops | bytes accessed | tf_op | source)
XLA Modules:
  0.0 760.8 jit_solution(4454899091737025960)
XLA Ops:
  6.5 0.0 copy-start
  6.5 0.0 reduce-scatter.2.cloned.1.call-start
  6.6 29.3 %all_gather.7 = bf16[64,2048]{1,0:T(8,128)(2,1)S(1)} all-gather(bf16[64,256]{1,0:T(8,128)(2,1)} %param.6), channel_id=1, replica_groups=mesh['row'=8,'col'=16] {'row'}, dimensions={1}, use_global_device_ids=true | all-gather | bytes 294912 | tf_op jit(solution)/shard_map/all_gather | solution.py:17
  35.8 27.8 %all_gather.6 = bf16[64,4096]{1,0:T(8,128)(2,1)S(1)} all-gather(bf16[64,256]{1,0:T(8,128)(2,1)} %param.6), channel_id=1, replica_groups=mesh['row'=8,'col'=16] {'col'}, dimensions={1}, use_global_device_ids=true | all-gather | bytes 557056 | tf_op jit(solution)/shard_map/all_gather | solution.py:14
  63.7 0.8 and_select_fusion.1
  64.4 0.1 copy.37
  64.5 0.1 copy.33
  64.6 0.1 copy.58
  64.6 0.1 copy.57
  64.7 11.9 %fusion.18 = f32[16,64,8,256]{3,1,2,0:T(8,128)} fusion(bf16[16,8,256,256]{3,2,1,0:T(8,128)(2,1)} %param.7, bf16[64,16,256,1]{2,1,0,3:T(8,128)(2,1)S(1)} %bitcast.59), kind=kOutput, calls=%fused_computation.22 | convolution fusion | flops 1073741824 | bytes 25690112 | tf_op jit(solution)/shard_map/ikab,cia->ckib/dot_general | solution.py:35
  76.6 14.1 %fusion = f32[8,64,16,256]{3,1,2,0:T(8,128)} fusion(bf16[16,8,256,256]{3,2,1,0:T(8,128)(2,1)} %param.7, bf16[64,8,256,1]{2,1,0,3:T(8,128)(2,1)S(1)} %bitcast.64), kind=kOutput, calls=%fused_computation | convolution fusion | flops 1073741824 | bytes 25427968 | tf_op jit(solution)/shard_map/ikab,ckb->cika/dot_general | solution.py:25
  90.7 0.0 copy-done
  90.7 0.7 fusion.11
  91.4 0.0 slice-start
  91.4 2.4 fusion.10
  93.9 0.0 copy-done.1
  93.9 0.0 slice-start.1
  93.9 4.8 fusion.3
  98.7 1.2 broadcast_select_fusion
  99.8 2.7 fusion.2
  102.5 0.2 fusion.14
  102.8 3.9 copy.59
  106.7 0.0 reduce-scatter.2.cloned.1.call-update
  106.7 647.2 %reduce-scatter.2.cloned.1.call-done = f32[64,256]{1,0:T(8,128)} async-done(((f32[64,32768]{1,0:T(8,128)}), f32[64,256]{1,0:T(8,128)}) %reduce-scatter.2.cloned.1.call-update) | async-done | bytes 65552 | tf_op jit(solution)/shard_map/reduce_scatter | solution.py:51
  (7 shorter events, 0.0 us)
Async XLA Ops:
  6.5 84.2 %copy-start = (bf16[16,8,32,256]{3,2,1,0:T(8,128)(2,1)S(1)}, bf16[16,8,32,256]{3,2,1,0:T(8,128)(2,1)}, u32[]{:S(2)}) copy-start(bf16[16,8,32,256]{3,2,1,0:T(8,128)(2,1)} %param.8) | copy-start | bytes 6291460
  6.5 747.4 %reduce-scatter.2.cloned.1.call-start = ((), (), s32[]{:S(2)}) async-start(), calls=%async_computation.1 | async-start | bytes 8454144 | tf_op jit(solution)/shard_map/reduce_scatter | solution.py:51
  90.7 3.2 copy-start.1
  91.4 8.4 %slice-start = ((s8[8388608]{0:T(1024)(128)(4,1)}), s8[4194304]{0:T(1024)(128)(4,1)S(1)}, s32[]{:S(2)}) async-start(s8[8388608]{0:T(1024)(128)(4,1)} %bitcast.56), calls=%async_computation.2 | async-start | bytes 8388608
  93.9 5.9 slice-start.1
Sparse Core Ops, SparseCore 0:
  106.9 647.0 reduce-scatter.1
where the time goes:
time: 761 us
  waiting for transfers between devices  647 us (85%)
  blocking collectives  57.1 us (8%)
  matrix products  36.5 us (5%)
  between operations  13.5 us (2%)
    reduce_scatter x1, waiting for transfers between devices, shards(): lax.psum_scatter(whole.reshape(num_cases, row_count * col_count * block_s...  647 us
    all_gather x1, blocking collectives, shards(): lax.all_gather(sources, 'row', axis=1, tiled=True)  29.3 us
    all_gather x1, blocking collectives, shards(): lax.all_gather(sources, 'col', axis=1, tiled=True)  27.8 us
  transfers between devices with their start and end apart: 1, of which 1 were waited for; matrix products, arithmetic and copies ran while one was open for 0% of the time, Pallas kernels for 0%

commit v1 on v0

--- a/solution.py
+++ b/solution.py
@@ -14,9 +14,9 @@
     row_src = lax.all_gather(sources, "col", axis=1, tiled=True).reshape(
         num_cases, col_count, block_size
     )
-    col_src = lax.all_gather(sources, "row", axis=1, tiled=True).reshape(
-        num_cases, row_count, block_size
-    )
+    col_src = jnp.concatenate(
+        lax.all_to_all(jnp.stack([sources] * lax.axis_size("row")), "row", 0, 0), axis=1
+    ).reshape(num_cases, row_count, block_size)
     row_ids = row_index * col_count + jnp.arange(col_count, dtype=jnp.int32)
     col_ids = jnp.arange(row_count, dtype=jnp.int32) * col_count + col_index
     live = (row_ids[:, None] <= col_ids[None, :]) & (col_ids[None, :] <= band_end[:, None])

time: 761 us -> 740 us (0.972)
  blocking collectives: 57.1 us -> 27.8 us
    all_gather x1 -> x0, blocking collectives: 29.3 us -> none  [shards(): lax.all_gather(sources, 'row', axis=1, tiled=True)]
  transfers between devices with their start and end apart: 1 -> 2, of which waited for: 1 -> 1; matrix products, arithmetic and copies ran while one was open for 0% -> 2% of each run, Pallas kernels for 0% -> 0%
where the time goes in v1:
time: 740 us
  waiting for transfers between devices  648 us (88%)
  matrix products  32.8 us (4%)
  blocking collectives  27.8 us (4%)
  between operations  13.5 us (2%)
    reduce_scatter x1, waiting for transfers between devices, shards(): lax.psum_scatter(whole.reshape(num_cases, row_count * col_count * block_s...  648 us
    all_gather x1, blocking collectives, shards(): lax.all_gather(sources, 'col', axis=1, tiled=True)  27.8 us
  transfers between devices with their start and end apart: 2, of which 1 were waited for; matrix products, arithmetic and copies ran while one was open for 2% of the time, Pallas kernels for 0%

profile of v1, /device:TPU:0, one launch (start us, length us, event | category | flops | bytes accessed | tf_op | source)
XLA Modules:
  0.0 740.1 jit_solution(15860736631817048677)
XLA Ops:
  6.5 0.0 copy-start
  6.5 1.7 stack.2
  8.2 5.4 all-to-all-start
  13.6 0.0 reduce-scatter.2.cloned.1.call-start
  13.7 27.8 %all_gather.3 = bf16[64,4096]{1,0:T(8,128)(2,1)S(1)} all-gather(bf16[64,256]{1,0:T(8,128)(2,1)} %param.6), channel_id=1, replica_groups=mesh['row'=8,'col'=16] {'col'}, dimensions={1}, use_global_device_ids=true | all-gather | bytes 557056 | tf_op jit(solution)/shard_map/all_gather | solution.py:14
  41.5 0.8 and_select_fusion.1
  42.3 0.1 copy.34
  42.4 0.1 copy.30
  42.4 0.1 copy.49
  42.5 0.0 copy-done
  42.5 0.7 fusion.11
  43.2 0.0 copy-start.2
  43.3 8.8 %fusion.18 = f32[16,64,8,256]{3,1,2,0:T(8,128)S(1)} fusion(bf16[16,8,256,256]{3,2,1,0:T(8,128)(2,1)} %param.7, bf16[64,16,256,1]{2,1,0,3:T(8,128)(2,1)S(1)} %bitcast.55), kind=kOutput, calls=%fused_computation.22 | convolution fusion | flops 1073741824 | bytes 25690112 | tf_op jit(solution)/shard_map/ikab,cia->ckib/dot_general | solution.py:35
  52.1 2.2 fusion.3
  54.3 4.3 broadcast_select_fusion
  58.6 0.0 all-to-all-done
  58.6 2.3 fusion.10
  60.9 14.1 %fusion = f32[8,64,16,256]{3,1,2,0:T(8,128)} fusion(bf16[16,8,256,256]{3,2,1,0:T(8,128)(2,1)} %param.7, bf16[8,64,256]{2,1,0:T(8,128)(2,1)S(1)} %all-to-all-done), kind=kOutput, calls=%fused_computation | convolution fusion | flops 1073741824 | bytes 25427968 | tf_op jit(solution)/shard_map/ikab,ckb->cika/dot_general | solution.py:25
  75.0 4.8 fusion.2
  79.8 1.1 copy-done.1
  80.8 0.2 fusion.14
  81.1 3.9 copy.50
  85.0 0.0 reduce-scatter.2.cloned.1.call-update
  85.0 648.3 %reduce-scatter.2.cloned.1.call-done = f32[64,256]{1,0:T(8,128)} async-done(((f32[64,32768]{1,0:T(8,128)}), f32[64,256]{1,0:T(8,128)}) %reduce-scatter.2.cloned.1.call-update) | async-done | bytes 65552 | tf_op jit(solution)/shard_map/reduce_scatter | solution.py:51
  (5 shorter events, 0.0 us)
Async XLA Ops:
  6.5 36.0 %copy-start = (bf16[16,8,32,256]{3,2,1,0:T(8,128)(2,1)S(1)}, bf16[16,8,32,256]{3,2,1,0:T(8,128)(2,1)}, u32[]{:S(2)}) copy-start(bf16[16,8,32,256]{3,2,1,0:T(8,128)(2,1)} %param.8) | copy-start | bytes 6291460
  8.2 50.4 %all-to-all-start = ((bf16[8,64,256]{2,1,0:T(8,128)(2,1)}), bf16[8,64,256]{2,1,0:T(8,128)(2,1)S(1)}, u32[]{:S(2)}, u32[]{:S(2)}) async-start(bf16[8,64,256]{2,1,0:T(8,128)(2,1)} %stack.2), calls=%async_computation | async-start | bytes 524288 | tf_op jit(solution)/shard_map/all_to_all | solution.py:18
  13.6 719.7 %reduce-scatter.2.cloned.1.call-start = ((), (), s32[]{:S(2)}) async-start(), calls=%async_computation.2 | async-start | bytes 8454144 | tf_op jit(solution)/shard_map/reduce_scatter | solution.py:51
  43.2 8.8 %copy-start.2 = (bf16[16,8,32,256]{3,2,1,0:T(8,128)(2,1)S(1)}, bf16[16,8,32,256]{3,2,1,0:T(8,128)(2,1)}, u32[]{:S(2)}) copy-start(bf16[16,8,32,256]{3,2,1,0:T(8,128)(2,1)} %param.9) | copy-start | bytes 6291460
  75.0 5.8 copy-start.1
Sparse Core Ops, SparseCore 0:
  85.1 648.0 reduce-scatter.1
